TPU v7x, 256 devices: a whole 4x4x8 slice. The times are simulated.
256 devices in a mesh: expert: 32 (over x, z), vocab: 8 (over y, core).
Axes of the slice: x: 4, y: 4, z: 8, core: 2. Of those that a mesh axis runs over, the one named last changes fastest.
Arguments:
- out_grad: bfloat16 [4096, 4096], P('expert', 'vocab'), may hold values from -6 to 6
- residual_stream: bfloat16 [4096, 4096], P('expert', 'vocab'), may hold values from -228 to 228
- norm_gain: float32 [4096], P('vocab'), may hold values from 0.25 to 51
- expert_ids: int32 [4096, 8], P('expert'), may hold values from 0 to 31, all different within a row; in each aligned block of 128 rows (0 to 127, 128 to 255, ...) at most 38 rows name the same one
- gate_scores: float32 [4096, 8], P('expert'), may hold values from 0.05 to 1
- saved_gate: bfloat16 [32, 1216, 1536], P('expert', None, 'vocab'), may hold values from -6 to 6
- saved_up: bfloat16 [32, 1216, 1536], P('expert', None, 'vocab'), may hold values from -6 to 6
- gate_weight: bfloat16 [32, 4096, 1536], P('expert', None, 'vocab'), may hold values from -0.09375 to 0.09375
- up_weight: bfloat16 [32, 4096, 1536], P('expert', None, 'vocab'), may hold values from -0.09375 to 0.09375
- down_weight: bfloat16 [32, 1536, 4096], P('expert', 'vocab'), may hold values from -0.15625 to 0.15625
- embedding: bfloat16 [98304, 4096], P(('expert', 'vocab')), may hold values from -0.09375 to 0.09375
- allowed: int32 [98304], P(('expert', 'vocab')), may hold values 0 or 1
- suffix_start: int32 [32], P('expert'), may hold values from 0 to 108
Outputs:
- token_grad: bfloat16 [4096, 4096], P('expert', 'vocab')
- scores: float32 [640, 98304], P(None, ('expert', 'vocab'))
Inputs may be any that keep to these rules, and one draw needn't show every extreme that they name: `expert_ids`: in each aligned block of 128 rows (one behavior) a row names 8 different experts and no expert is named by more than 38 rows; some expert is named by exactly 38 rows in some blocks.
All inputs are finite; a program needn't handle non-finite values. No bound on the sum of `allowed` on one device may be relied on, other than what follows from the above.
Results may differ from a plain program's by a relative error of at most 0.01.
Values may be sent and summed in bfloat16 or wider, within the bound.
No kernel may reach another device: no remote copies, remote signals or barrier semaphores. Data moves between devices by JAX's collectives and lax.ppermute only.
A program may use at most 128 MiB of HBM per device.

v0:
```python
import jax
import jax.numpy as jnp
from jax import lax
from jax.sharding import PartitionSpec as P

D = 4096
SUFFIX = 20


def sent_to_all(value, axis):
    peers = lax.axis_size(axis)
    return lax.all_to_all(
        jnp.broadcast_to(value[None], (peers, *value.shape)), axis, 0, 0, tiled=True
    )


def taken_together(value, axis):
    everything = sent_to_all(value, axis)
    return jnp.sum(everything, axis=0)


def in_order(parts, dim):
    parts = jnp.moveaxis(parts, 0, dim)
    lengths = parts.shape
    return parts.reshape(*lengths[:dim], lengths[dim] * lengths[dim + 1], *lengths[dim + 2 :])


def collect(value, axis, dim):
    return in_order(sent_to_all(value, axis), dim)


def shards(
    out_grad,
    residual_stream,
    norm_gain,
    expert_ids,
    gate_scores,
    saved_gate,
    saved_up,
    gate_weight,
    up_weight,
    down_weight,
    embedding,
    allowed,
    suffix_start,
):
    n_expert = lax.axis_size("expert")
    seq_len, d_slice = out_grad.shape
    top_k = expert_ids.shape[1]
    slot_count = saved_gate.shape[1]
    capacity = slot_count // n_expert
    contract = (((1,), (1,)), ((), ()))
    chosen = expert_ids.reshape(-1)
    matches = (chosen[:, None] == jnp.arange(n_expert, dtype=jnp.int32)[None, :]).astype(jnp.int32)
    before = jnp.cumsum(matches, axis=0) - matches
    position = jnp.sum(before * matches, axis=1)
    target = chosen * capacity + position
    gate_share = gate_scores / jnp.sum(gate_scores, axis=1, keepdims=True)
    routed = (gate_share[:, :, None] * out_grad.astype(jnp.float32)[:, None, :]).astype(
        jnp.bfloat16
    )
    routed = routed.reshape(seq_len * top_k, d_slice)
    buffer = jnp.zeros((slot_count, d_slice), jnp.bfloat16).at[target].set(routed)
    arrived = lax.all_to_all(buffer, "expert", split_axis=0, concat_axis=0, tiled=True)
    incoming = lax.all_gather(arrived, "vocab", axis=1, tiled=True)
    act_grad = lax.dot_general(
        incoming, down_weight[0], contract, preferred_element_type=jnp.float32
    )
    pre_gate = saved_gate[0].astype(jnp.float32)
    pre_up = saved_up[0].astype(jnp.float32)
    sigmoid_g = jax.nn.sigmoid(pre_gate)
    gate_grad = (act_grad * pre_up * sigmoid_g * (1.0 + pre_gate * (1.0 - sigmoid_g))).astype(
        jnp.bfloat16
    )
    up_grad = (act_grad * pre_gate * sigmoid_g).astype(jnp.bfloat16)
    partial_value = lax.dot_general(
        gate_grad, gate_weight[0], contract, preferred_element_type=jnp.float32
    )
    partial_value = partial_value + lax.dot_general(
        up_grad, up_weight[0], contract, preferred_element_type=jnp.float32
    )
    partial_rounded = partial_value.astype(jnp.bfloat16)
    slot_grad = lax.psum_scatter(partial_rounded, "vocab", scatter_dimension=1, tiled=True).astype(
        jnp.float32
    )
    returned = lax.all_to_all(
        slot_grad.astype(jnp.bfloat16), "expert", split_axis=0, concat_axis=0, tiled=True
    ).astype(slot_grad.dtype)
    moe_grad = jnp.sum(returned[target].reshape(seq_len, top_k, d_slice), axis=1)
    resid = residual_stream.astype(jnp.float32)
    sum_squares = taken_together(jnp.sum(resid * resid, axis=1), "vocab")
    inverse = lax.rsqrt(sum_squares / D + 1e-06)
    normed = resid * inverse[:, None]
    scaled = moe_grad * norm_gain[None, :]
    row_project = taken_together(jnp.sum(scaled * normed, axis=1), "vocab") / D
    token_grad = (
        out_grad.astype(jnp.float32) + inverse[:, None] * (scaled - normed * row_project[:, None])
    ).astype(jnp.bfloat16)
    suffix_grad = lax.dynamic_slice_in_dim(token_grad, suffix_start[0], SUFFIX, 0)
    suffix_grad = collect(suffix_grad, "vocab", 1)
    raw_scores = -lax.dot_general(
        lax.all_gather(suffix_grad, "expert", axis=0, tiled=True),
        embedding,
        contract,
        preferred_element_type=jnp.float32,
    )
    scores = jnp.where(allowed[None, :] > 0, raw_scores, jnp.float32(0.0))
    return (token_grad, scores)


def solution(mesh):
    placed = (
        P("expert", "vocab"),
        P("expert", "vocab"),
        P("vocab"),
        P("expert", None),
        P("expert", None),
        P("expert", None, "vocab"),
        P("expert", None, "vocab"),
        P("expert", None, "vocab"),
        P("expert", None, "vocab"),
        P("expert", "vocab", None),
        P(("expert", "vocab"), None),
        P(("expert", "vocab")),
        P("expert"),
    )
    return jax.shard_map(
        shards,
        mesh=mesh,
        in_specs=placed,
        out_specs=(P("expert", "vocab"), P(None, ("expert", "vocab"))),
        check_vma=False,
    )
```

profile of v0, /device:TPU:8, one launch (start us, length us, event | category | flops | bytes accessed | tf_op | source)
XLA Modules:
  0.0 413.3 jit_solution(6126934621142170420)
XLA Ops:
  7.2 0.0 copy-start
  7.2 0.0 all-gather.4.cloned.1.call-start
  7.2 0.9 copy.37
  8.2 0.1 eq.29
  8.3 0.1 eq.25
  8.3 0.7 broadcast_multiply_fusion
  9.1 9.0 %reduce-window.6 = s32[32,8,128]{2,1,0:T(8,128)S(1)} reduce-window(s32[32,8,128]{2,1,0:T(8,128)S(1)} %fusion.39, s32[]{:T(128)} %constant.7.clone.1), window={size=1x1x128 pad=0_0x0_0x127_0}, to_apply=%region_2.3 | reduce-window | flops 4161536 | bytes 262148 | tf_op jit(solution)/shard_map/reduce-window
  18.1 0.1 slice.10
  18.2 0.1 copy.39
  18.3 0.1 copy.40
  18.4 0.1 broadcast_add_fusion
  18.5 0.1 copy.36
  18.6 0.1 mul.95
  18.7 0.9 convert_element_type.50
  19.7 0.7 reduce_sum.69
  20.4 0.7 broadcast_divide_fusion
  21.0 0.7 copy.41
  21.8 0.9 mul.97
  22.8 6.6 %scatter_custom_fusion = bf16[1216,512]{1,0:T(8,128)(2,1)} fusion(s32[1024]{0:T(1024)S(1)} %bitcast.66, f32[128,512]{1,0:T(8,128)S(1)} %convert_element_type.50, f32[1024]{0:T(1024)S(1)} %mul.97, bf16[]{:T(256)} %constant.5.clone.1), kind=kCustom, calls=%fused_computation.16 | custom fusion | flops 1048576 | bytes 1511426 | tf_op jit(solution)/shard_map/scatter | solution.py:63
  29.4 2.3 all_to_all.26
  31.7 46.4 %all_to_all.38 = bf16[32,38,512]{2,1,0:T(8,128)(2,1)} all-to-all(bf16[32,38,512]{2,1,0:T(8,128)(2,1)} %all_to_all.26), channel_id=1, replica_groups=mesh['expert'=32,'vocab'=8] {'expert'}, dimensions={0} | all-to-all | bytes 2490368 | tf_op jit(solution)/shard_map/all_to_all | solution.py:64
  78.1 2.3 all_to_all.28
  80.4 0.0 all-gather.4.cloned.1.call-update
  80.4 0.0 reduce-scatter.2.cloned.1.call-start
  80.4 54.2 %all-gather.4.cloned.1.call-done = bf16[1216,4096]{1,0:T(8,128)(2,1)} async-done(((bf16[1216,512]{1,0:T(8,128)(2,1)}), bf16[1216,4096]{1,0:T(8,128)(2,1)}) %all-gather.4.cloned.1.call-update) | async-done | bytes 9961488 | tf_op jit(solution)/shard_map/all_gather | solution.py:65
  134.6 7.6 %fusion.4 = f32[1216,192]{0,1:T(8,128)S(1)} fusion(bf16[1216,4096]{1,0:T(8,128)(2,1)} %all-gather.4.cloned.1.call-done, bf16[1,192,4096]{2,1,0:T(8,128)(2,1)} %param.22), kind=kOutput, calls=%fused_computation.9 | convolution fusion | flops 1912602624 | bytes 12468224 | tf_op jit(solution)/shard_map/dot_general | solution.py:66
  142.2 0.0 copy-start.1
  142.2 0.9 copy-done.1
  143.2 0.0 copy-done.2
  143.2 0.0 copy-done.3
  143.2 0.0 copy-done.5
  143.2 8.4 %fusion.2 = f32[1216,4096]{1,0:T(8,128)} fusion(bf16[1,4096,192]{1,2,0:T(8,128)(2,1)S(1)} %copy-done.3, f32[1216,192]{0,1:T(8,128)S(1)} %fusion.4, bf16[1,1216,192]{1,2,0:T(8,128)(2,1)S(1)} %copy-done.5, bf16[1,1216,192]{1,2,0:T(8,128)(2,1)S(1)} %copy-done.2), kind=kOutput, calls=%fused_computation.7 | convolution fusion | flops 1915404288 | bytes 23363584 | tf_op jit(solution)/shard_map/dot_general | solution.py:76
  151.6 14.2 %add_convert_fusion = bf16[1216,4096]{1,0:T(8,128)(2,1)} fusion(f32[1216,4096]{1,0:T(8,128)} %fusion.2, bf16[1,4096,192]{1,2,0:T(8,128)(2,1)} %param.21, f32[1216,192]{0,1:T(8,128)} %copy-done.1, bf16[1,1216,192]{1,2,0:T(8,128)(2,1)} %param.18), kind=kOutput, calls=%fused_computation.2 | convolution fusion | flops 1924198400 | bytes 32858112 | tf_op jit(solution)/shard_map/dot_general | solution.py:79
  165.7 0.0 reduce-scatter.2.cloned.1.call-update
  165.7 0.9 copy-done.4
  166.6 0.1 fusion.35
  166.7 0.6 broadcast_in_dim.16
  167.3 4.5 %all-to-all-start = ((f32[8,1,128]{2,1,0:T(1,128)}), f32[8,1,128]{2,1,0:T(1,128)S(1)}, u32[]{:S(2)}, u32[]{:S(2)}) async-start(f32[8,1,128]{2,1,0:T(1,128)} %broadcast_in_dim.16), calls=%async_computation | async-start | bytes 8192 | tf_op jit(solution)/shard_map/all_to_all | solution.py:12
  171.9 55.1 %reduce-scatter.2.cloned.1.call-done = bf16[1216,512]{1,0:T(8,128)(2,1)} async-done(((bf16[1216,4096]{1,0:T(8,128)(2,1)}), bf16[1216,512]{1,0:T(8,128)(2,1)}) %reduce-scatter.2.cloned.1.call-update) | async-done | bytes 1245200 | tf_op jit(solution)/shard_map/reduce_scatter | solution.py:83
  227.0 2.3 all_to_all.29
  229.3 0.0 all-to-all-done
  229.3 10.2 %all-to-all-start.2 = ((bf16[32,38,512]{2,1,0:T(8,128)(2,1)}), bf16[32,38,512]{2,1,0:T(8,128)(2,1)}, u32[]{:S(2)}, u32[]{:S(2)}) async-start(bf16[32,38,512]{2,1,0:T(8,128)(2,1)} %all_to_all.29), calls=%async_computation.3 | async-start | bytes 2621440 | tf_op jit(solution)/shard_map/all_to_all | solution.py:86
  239.5 34.5 %all-to-all-done.2 = bf16[32,38,512]{2,1,0:T(8,128)(2,1)} async-done(((bf16[32,38,512]{2,1,0:T(8,128)(2,1)}), bf16[32,38,512]{2,1,0:T(8,128)(2,1)}, u32[]{:S(2)}, u32[]{:S(2)}) %all-to-all-start.2) | async-done | bytes 1245216 | tf_op jit(solution)/shard_map/all_to_all | solution.py:86
  274.0 2.7 reshape.102
  276.7 7.0 %gather_fusion = f32[1024,512]{1,0:T(8,128)} fusion(f32[1216,512]{1,0:T(8,128)} %reshape.102, s32[1024]{0:T(1024)S(1)} %broadcast_clamp_fusion), kind=kCustom, calls=%fused_computation | custom fusion | bytes 4198400 | tf_op jit(solution)/shard_map/gather | solution.py:89
  283.6 2.1 bitcast_reduce_fusion
  285.8 0.0 copy-done.7
  285.8 0.2 fusion.30
  286.0 0.6 broadcast_in_dim.18
  286.6 5.1 %all-to-all-start.3 = ((f32[8,1,128]{2,1,0:T(1,128)}), f32[8,1,128]{2,1,0:T(1,128)S(1)}, u32[]{:S(2)}, u32[]{:S(2)}) async-start(f32[8,1,128]{2,1,0:T(1,128)} %broadcast_in_dim.18), calls=%async_computation.4 | async-start | bytes 8192 | tf_op jit(solution)/shard_map/all_to_all | solution.py:12
  291.7 0.0 all-gather.6.cloned.1.call-start
  292.4 3.1 all-to-all-done.3
  295.5 0.5 reduce_sum.72
  296.0 0.7 broadcast_multiply_fusion.1
  296.6 1.1 fusion.34
  297.7 0.0 copy-start.6
  297.8 9.2 %all_to_all.39 = bf16[8,20,512]{2,1,0:T(8,128)(2,1)S(1)} all-to-all(bf16[8,20,512]{2,1,0:T(8,128)(2,1)S(1)} %broadcast_in_dim.20), channel_id=1, replica_groups=mesh['expert'=32,'vocab'=8] {'vocab'}, dimensions={0} | all-to-all | bytes 327680 | tf_op jit(solution)/shard_map/all_to_all | solution.py:12
  307.0 0.1 copy.43
  307.0 0.8 reshape.119
  307.8 0.0 all-gather.6.cloned.1.call-update
  307.8 0.0 copy-done.8
  307.9 84.7 %all-gather.6.cloned.1.call-done = bf16[32,20,4096]{2,1,0:T(8,128)(2,1)} async-done(((bf16[1,20,4096]{2,1,0:T(8,128)(2,1)}), bf16[32,20,4096]{2,1,0:T(8,128)(2,1)}) %all-gather.6.cloned.1.call-update) | async-done | bytes 5242896 | tf_op jit(solution)/shard_map/all_gather | solution.py:102
  392.6 7.8 %reshape.120 = bf16[640,4096]{1,0:T(8,128)(2,1)} reshape(bf16[32,20,4096]{2,1,0:T(8,128)(2,1)} %all-gather.6.cloned.1.call-done) | data formatting | bytes 10485760
  400.4 6.3 %fusion.6 = f32[640,384]{1,0:T(8,128)} fusion(bf16[640,4096]{1,0:T(8,128)(2,1)} %reshape.120, bf16[384,4096]{1,0:T(8,128)(2,1)S(1)} %copy-done, pred[384]{0:T(512)(128)(4,1)S(1)} %broadcast_compare_fusion), kind=kOutput, calls=%fused_computation.15 | convolution fusion | flops 2013757440 | bytes 9372032 | tf_op jit(solution)/shard_map/dot_general | solution.py:101
  (19 shorter events, 0.2 us)
Async XLA Ops:
  7.2 393.3 %copy-start = (bf16[384,4096]{1,0:T(8,128)(2,1)S(1)}, bf16[384,4096]{1,0:T(8,128)(2,1)}, u32[]{:S(2)}) copy-start(bf16[384,4096]{1,0:T(8,128)(2,1)} %param.23) | copy-start | bytes 9437188
  7.2 127.4 %all-gather.4.cloned.1.call-start = ((), (), s32[]{:S(2)}) async-start(), calls=%async_computation.6 | async-start | bytes 11206656 | tf_op jit(solution)/shard_map/all_gather | solution.py:65
  80.4 146.6 %reduce-scatter.2.cloned.1.call-start = ((), (), s32[]{:S(2)}) async-start(), calls=%async_computation.7 | async-start | bytes 11206656 | tf_op jit(solution)/shard_map/reduce_scatter | solution.py:83
  134.6 8.6 %copy-start.2 = (bf16[1,1216,192]{1,2,0:T(8,128)(2,1)S(1)}, bf16[1,1216,192]{1,2,0:T(8,128)(2,1)}, u32[]{:S(2)}) copy-start(bf16[1,1216,192]{1,2,0:T(8,128)(2,1)} %param.18) | copy-start | bytes 1400836
  134.6 8.6 %copy-start.3 = (bf16[1,4096,192]{1,2,0:T(8,128)(2,1)S(1)}, bf16[1,4096,192]{1,2,0:T(8,128)(2,1)}, u32[]{:S(2)}) copy-start(bf16[1,4096,192]{1,2,0:T(8,128)(2,1)} %param.20) | copy-start | bytes 4718596
  134.6 8.6 %copy-start.5 = (bf16[1,1216,192]{1,2,0:T(8,128)(2,1)S(1)}, bf16[1,1216,192]{1,2,0:T(8,128)(2,1)}, u32[]{:S(2)}) copy-start(bf16[1,1216,192]{1,2,0:T(8,128)(2,1)} %param.19) | copy-start | bytes 1400836
  142.2 0.9 copy-start.1
  165.7 0.9 copy-start.4
  167.3 62.0 %all-to-all-start = ((f32[8,1,128]{2,1,0:T(1,128)}), f32[8,1,128]{2,1,0:T(1,128)S(1)}, u32[]{:S(2)}, u32[]{:S(2)}) async-start(f32[8,1,128]{2,1,0:T(1,128)} %broadcast_in_dim.16), calls=%async_computation | async-start | bytes 8192 | tf_op jit(solution)/shard_map/all_to_all | solution.py:12
  229.3 44.7 %all-to-all-start.2 = ((bf16[32,38,512]{2,1,0:T(8,128)(2,1)}), bf16[32,38,512]{2,1,0:T(8,128)(2,1)}, u32[]{:S(2)}, u32[]{:S(2)}) async-start(bf16[32,38,512]{2,1,0:T(8,128)(2,1)} %all_to_all.29), calls=%async_computation.3 | async-start | bytes 2621440 | tf_op jit(solution)/shard_map/all_to_all | solution.py:86
  283.6 2.1 copy-start.7
  283.6 24.2 %copy-start.8 = (s32[384]{0:T(512)S(1)}, s32[384]{0:T(512)}, u32[]{:S(2)}) copy-start(s32[384]{0:T(512)} %param.24) | copy-start | bytes 4612
  286.6 8.9 %all-to-all-start.3 = ((f32[8,1,128]{2,1,0:T(1,128)}), f32[8,1,128]{2,1,0:T(1,128)S(1)}, u32[]{:S(2)}, u32[]{:S(2)}) async-start(f32[8,1,128]{2,1,0:T(1,128)} %broadcast_in_dim.18), calls=%async_computation.4 | async-start | bytes 8192 | tf_op jit(solution)/shard_map/all_to_all | solution.py:12
  291.7 100.9 %all-gather.6.cloned.1.call-start = ((), (), s32[]{:S(2)}) async-start(), calls=%async_computation.8 | async-start | bytes 6488064 | tf_op jit(solution)/shard_map/all_gather | solution.py:102
  297.7 9.3 %copy-start.6 = (bf16[128,512]{1,0:T(8,128)(2,1)}, bf16[128,512]{1,0:T(8,128)(2,1)S(1)}, u32[]{:S(2)}) copy-start(bf16[128,512]{1,0:T(8,128)(2,1)S(1)} %fusion.34) | copy-start | bytes 393220
Sparse Core Ops, SparseCore 0:
  80.5 54.0 all-gather.3
  165.9 61.0 reduce-scatter.1
  308.0 84.5 all-gather.5
where the time goes:
time: 414 us; the launch traced here: 413 us
  waiting for transfers between devices  232 us (56%)
  blocking collectives  55.6 us (13%)
  matrix products  36.5 us (9%)
  local copies, waits for them, and re-layouts  31.6 us (8%)
  other arithmetic  23.5 us (6%)
  starting transfers between devices  19.9 us (5%)
  between operations  14.6 us (4%)
    all_gather x1, waiting for transfers between devices, shards(): lax.all_gather(suffix_grad, 'expert', axis=0, tiled=True)  84.7 us
    reduce_scatter x1, waiting for transfers between devices, shards(): lax.psum_scatter(partial_rounded, 'vocab', scatter_dimension=1, tiled=True)  55.1 us
    all_gather x1, waiting for transfers between devices, shards(): incoming = lax.all_gather(arrived, 'vocab', axis=1, tiled=True)  54.2 us
    all_to_all x1, blocking collectives, shards(): lax.all_to_all(buffer, 'expert', split_axis=0, concat_axis=0, tiled=True)  46.4 us
    all_to_all x1, waiting for transfers between devices, shards(): lax.all_to_all(slot_grad.astype(jnp.bfloat16), 'expert', split_axis=0, co...  34.5 us
    dot_general x1, matrix products, shards(): lax.dot_general(up_grad, up_weight[0], contract, preferred_element_type=j...  14.2 us
    unnamed x21, local copies, waits for them, and re-layouts  11.4 us
    all_to_all x1, starting transfers between devices, shards(): lax.all_to_all(slot_grad.astype(jnp.bfloat16), 'expert', split_axis=0, co...  10.2 us
  transfers between devices with their start and end apart: 6, of which 5 were waited for; matrix products, arithmetic and copies ran while one was open for 0% of the time, Pallas kernels for 0%

commit v1 on v0

--- a/solution.py
+++ b/solution.py
@@ -5,6 +5,12 @@
 
 D = 4096
 SUFFIX = 20
+
+
+def gather_by_exchange(x, axis, dim):
+    count = lax.axis_size(axis)
+    repeats = [count if d == dim else 1 for d in range(x.ndim)]
+    return lax.all_to_all(jnp.tile(x, repeats), axis, split_axis=dim, concat_axis=dim, tiled=True)
 
 
 def sent_to_all(value, axis):
@@ -99,7 +105,7 @@
     suffix_grad = lax.dynamic_slice_in_dim(token_grad, suffix_start[0], SUFFIX, 0)
     suffix_grad = collect(suffix_grad, "vocab", 1)
     raw_scores = -lax.dot_general(
-        lax.all_gather(suffix_grad, "expert", axis=0, tiled=True),
+        gather_by_exchange(suffix_grad, "expert", 0),
         embedding,
         contract,
         preferred_element_type=jnp.float32,

time: 414 us -> 479 us (1.16)
  waiting for transfers between devices: 232 us -> 288 us
  starting transfers between devices: 19.9 us -> 26 us
    all_to_all x0 -> x1, waiting for transfers between devices: none -> 141 us  [gather_by_exchange(): lax.all_to_all(jnp.tile(x, repeats), axis, split_axis=dim, concat_axis=di...]
    all_gather x1 -> x0, waiting for transfers between devices: 84.7 us -> none  [shards(): lax.all_gather(suffix_grad, 'expert', axis=0, tiled=True)]
    unnamed x21, local copies, waits for them, and re-layouts: 11.4 us -> 2.87 us
    all_to_all x0 -> x1, local copies, waits for them, and re-layouts: none -> 7.84 us  [gather_by_exchange(): lax.all_to_all(jnp.tile(x, repeats), axis, split_axis=dim, concat_axis=di...]
    all_to_all x0 -> x1, starting transfers between devices: none -> 6.05 us  [gather_by_exchange(): lax.all_to_all(jnp.tile(x, repeats), axis, split_axis=dim, concat_axis=di...]
where the time goes in v1:
time: 479 us; the launch traced here: 477 us
  waiting for transfers between devices  288 us (60%)
  blocking collectives  55.6 us (12%)
  matrix products  36.5 us (8%)
  local copies, waits for them, and re-layouts  34.3 us (7%)
  starting transfers between devices  26 us (5%)
  other arithmetic  22.3 us (5%)
  between operations  14.9 us (3%)
    all_to_all x1, waiting for transfers between devices, gather_by_exchange(): lax.all_to_all(jnp.tile(x, repeats), axis, split_axis=dim, concat_axis=di...  141 us
    reduce_scatter x1, waiting for transfers between devices, shards(): lax.psum_scatter(partial_rounded, 'vocab', scatter_dimension=1, tiled=True)  55.1 us
    all_gather x1, waiting for transfers between devices, shards(): incoming = lax.all_gather(arrived, 'vocab', axis=1, tiled=True)  54.2 us
    all_to_all x1, blocking collectives, shards(): lax.all_to_all(buffer, 'expert', split_axis=0, concat_axis=0, tiled=True)  46.4 us
    all_to_all x1, waiting for transfers between devices, shards(): lax.all_to_all(slot_grad.astype(jnp.bfloat16), 'expert', split_axis=0, co...  34.5 us
    dot_general x1, matrix products, shards(): lax.dot_general(up_grad, up_weight[0], contract, preferred_element_type=j...  14.2 us
    all_to_all x1, starting transfers between devices, shards(): lax.all_to_all(slot_grad.astype(jnp.bfloat16), 'expert', split_axis=0, co...  10.2 us
    all_to_all x2, starting transfers between devices, sent_to_all(): lax.all_to_all(jnp.broadcast_to(value[None], (peers, *value.shape)), axis...  9.67 us
  transfers between devices with their start and end apart: 6, of which 5 were waited for; matrix products, arithmetic and copies ran while one was open for 0% of the time, Pallas kernels for 0%

profile of v1, /device:TPU:8, one launch (start us, length us, event | category | flops | bytes accessed | tf_op | source)
XLA Modules:
  0.0 477.1 jit_solution(7408411396727869910)
XLA Ops:
  7.2 0.0 copy-start
  7.2 0.0 all-gather.2.cloned.1.call-start
  7.2 0.9 copy.37
  8.2 0.1 eq.29
  8.3 0.1 eq.25
  8.3 0.7 broadcast_multiply_fusion
  9.1 9.0 %reduce-window.6 = s32[32,8,128]{2,1,0:T(8,128)S(1)} reduce-window(s32[32,8,128]{2,1,0:T(8,128)S(1)} %fusion.39, s32[]{:T(128)} %constant.7.clone.1), window={size=1x1x128 pad=0_0x0_0x127_0}, to_apply=%region_2.3 | reduce-window | flops 4161536 | bytes 262148 | tf_op jit(solution)/shard_map/reduce-window
  18.1 0.1 slice.10
  18.2 0.1 copy.39
  18.3 0.1 copy.40
  18.4 0.1 broadcast_add_fusion
  18.5 0.1 copy.36
  18.6 0.1 mul.95
  18.7 0.9 convert_element_type.50
  19.7 0.7 reduce_sum.69
  20.4 0.7 broadcast_divide_fusion
  21.0 0.7 copy.41
  21.8 0.9 mul.97
  22.8 6.6 %scatter_custom_fusion = bf16[1216,512]{1,0:T(8,128)(2,1)} fusion(s32[1024]{0:T(1024)S(1)} %bitcast.71, f32[128,512]{1,0:T(8,128)S(1)} %convert_element_type.50, f32[1024]{0:T(1024)S(1)} %mul.97, bf16[]{:T(256)} %constant.5.clone.1), kind=kCustom, calls=%fused_computation.16 | custom fusion | flops 1048576 | bytes 1511426 | tf_op jit(solution)/shard_map/scatter | solution.py:69
  29.4 2.3 all_to_all.32
  31.7 46.4 %all_to_all.47 = bf16[32,38,512]{2,1,0:T(8,128)(2,1)} all-to-all(bf16[32,38,512]{2,1,0:T(8,128)(2,1)} %all_to_all.32), channel_id=1, replica_groups=mesh['expert'=32,'vocab'=8] {'expert'}, dimensions={0} | all-to-all | bytes 2490368 | tf_op jit(solution)/shard_map/all_to_all | solution.py:70
  78.1 2.3 all_to_all.34
  80.4 0.0 all-gather.2.cloned.1.call-update
  80.4 0.0 reduce-scatter.2.cloned.1.call-start
  80.4 54.2 %all-gather.2.cloned.1.call-done = bf16[1216,4096]{1,0:T(8,128)(2,1)} async-done(((bf16[1216,512]{1,0:T(8,128)(2,1)}), bf16[1216,4096]{1,0:T(8,128)(2,1)}) %all-gather.2.cloned.1.call-update) | async-done | bytes 9961488 | tf_op jit(solution)/shard_map/all_gather | solution.py:71
  134.6 7.6 %fusion.4 = f32[1216,192]{0,1:T(8,128)S(1)} fusion(bf16[1216,4096]{1,0:T(8,128)(2,1)} %all-gather.2.cloned.1.call-done, bf16[1,192,4096]{2,1,0:T(8,128)(2,1)} %param.22), kind=kOutput, calls=%fused_computation.9 | convolution fusion | flops 1912602624 | bytes 12468224 | tf_op jit(solution)/shard_map/dot_general | solution.py:72
  142.2 0.0 copy-start.1
  142.2 0.9 copy-done.1
  143.2 0.0 copy-done.2
  143.2 0.0 copy-done.3
  143.2 0.0 copy-done.5
  143.2 8.4 %fusion.2 = f32[1216,4096]{1,0:T(8,128)} fusion(bf16[1,4096,192]{1,2,0:T(8,128)(2,1)S(1)} %copy-done.3, f32[1216,192]{0,1:T(8,128)S(1)} %fusion.4, bf16[1,1216,192]{1,2,0:T(8,128)(2,1)S(1)} %copy-done.5, bf16[1,1216,192]{1,2,0:T(8,128)(2,1)S(1)} %copy-done.2), kind=kOutput, calls=%fused_computation.7 | convolution fusion | flops 1915404288 | bytes 23363584 | tf_op jit(solution)/shard_map/dot_general | solution.py:82
  151.6 14.2 %add_convert_fusion = bf16[1216,4096]{1,0:T(8,128)(2,1)} fusion(f32[1216,4096]{1,0:T(8,128)} %fusion.2, bf16[1,4096,192]{1,2,0:T(8,128)(2,1)} %param.21, f32[1216,192]{0,1:T(8,128)} %copy-done.1, bf16[1,1216,192]{1,2,0:T(8,128)(2,1)} %param.18), kind=kOutput, calls=%fused_computation.2 | convolution fusion | flops 1924198400 | bytes 32858112 | tf_op jit(solution)/shard_map/dot_general | solution.py:85
  165.7 0.0 reduce-scatter.2.cloned.1.call-update
  165.7 0.9 copy-done.4
  166.6 0.1 fusion.35
  166.7 0.6 broadcast_in_dim.16
  167.3 4.5 all-to-all-start
  171.9 55.1 %reduce-scatter.2.cloned.1.call-done = bf16[1216,512]{1,0:T(8,128)(2,1)} async-done(((bf16[1216,4096]{1,0:T(8,128)(2,1)}), bf16[1216,512]{1,0:T(8,128)(2,1)}) %reduce-scatter.2.cloned.1.call-update) | async-done | bytes 1245200 | tf_op jit(solution)/shard_map/reduce_scatter | solution.py:89
  227.0 2.3 all_to_all.35
  229.3 0.0 all-to-all-done
  229.3 10.2 %all-to-all-start.2 = ((bf16[32,38,512]{2,1,0:T(8,128)(2,1)}), bf16[32,38,512]{2,1,0:T(8,128)(2,1)}, u32[]{:S(2)}, u32[]{:S(2)}) async-start(bf16[32,38,512]{2,1,0:T(8,128)(2,1)} %all_to_all.35), calls=%async_computation.3 | async-start | bytes 2621440 | tf_op jit(solution)/shard_map/all_to_all | solution.py:92
  239.5 34.5 %all-to-all-done.2 = bf16[32,38,512]{2,1,0:T(8,128)(2,1)} async-done(((bf16[32,38,512]{2,1,0:T(8,128)(2,1)}), bf16[32,38,512]{2,1,0:T(8,128)(2,1)}, u32[]{:S(2)}, u32[]{:S(2)}) %all-to-all-start.2) | async-done | bytes 1245216 | tf_op jit(solution)/shard_map/all_to_all | solution.py:92
  274.0 2.7 reshape.105
  276.7 7.0 %gather_fusion = f32[1024,512]{1,0:T(8,128)} fusion(f32[1216,512]{1,0:T(8,128)} %reshape.105, s32[1024]{0:T(1024)S(1)} %broadcast_clamp_fusion), kind=kCustom, calls=%fused_computation | custom fusion | bytes 4198400 | tf_op jit(solution)/shard_map/gather | solution.py:95
  283.6 2.1 bitcast_reduce_fusion
  285.7 0.0 copy-done.7
  285.8 0.2 fusion.30
  285.9 0.6 broadcast_in_dim.18
  286.5 5.1 %all-to-all-start.3 = ((f32[8,1,128]{2,1,0:T(1,128)}), f32[8,1,128]{2,1,0:T(1,128)S(1)}, u32[]{:S(2)}, u32[]{:S(2)}) async-start(f32[8,1,128]{2,1,0:T(1,128)} %broadcast_in_dim.18), calls=%async_computation.4 | async-start | bytes 8192 | tf_op jit(solution)/shard_map/all_to_all | solution.py:18
  292.3 3.1 all-to-all-done.3
  295.5 1.1 fusion.34
  296.5 0.0 copy-start.6
  296.6 9.2 %all_to_all.48 = bf16[8,20,512]{2,1,0:T(8,128)(2,1)S(1)} all-to-all(bf16[8,20,512]{2,1,0:T(8,128)(2,1)S(1)} %broadcast_in_dim.20), channel_id=1, replica_groups=mesh['expert'=32,'vocab'=8] {'vocab'}, dimensions={0} | all-to-all | bytes 327680 | tf_op jit(solution)/shard_map/all_to_all | solution.py:18
  305.8 0.1 copy.43
  305.9 0.1 copy.45
  305.9 0.0 copy-done.6
  306.0 3.4 tile.9
  309.4 6.0 %all-to-all-start.5 = ((bf16[32,20,4096]{2,1,0:T(8,128)(2,1)}), bf16[32,20,4096]{2,1,0:T(8,128)(2,1)}, u32[]{:S(2)}, u32[]{:S(2)}) async-start(bf16[32,20,4096]{2,1,0:T(8,128)(2,1)} %tile.9), calls=%async_computation.6 | async-start | bytes 12582912 | tf_op jit(solution)/shard_map/all_to_all | solution.py:13
  315.4 0.0 copy-done.8
  315.5 140.7 %all-to-all-done.5 = bf16[32,20,4096]{2,1,0:T(8,128)(2,1)} async-done(((bf16[32,20,4096]{2,1,0:T(8,128)(2,1)}), bf16[32,20,4096]{2,1,0:T(8,128)(2,1)}, u32[]{:S(2)}, u32[]{:S(2)}) %all-to-all-start.5) | async-done | bytes 5242912 | tf_op jit(solution)/shard_map/all_to_all | solution.py:13
  456.1 7.8 %all_to_all.40 = bf16[640,4096]{1,0:T(8,128)(2,1)} reshape(bf16[32,20,4096]{2,1,0:T(8,128)(2,1)} %all-to-all-done.5) | data formatting | bytes 10485760 | tf_op jit(solution)/shard_map/all_to_all | solution.py:13
  464.0 0.0 copy-done
  464.0 6.3 %fusion.6 = f32[640,384]{1,0:T(8,128)} fusion(bf16[640,4096]{1,0:T(8,128)(2,1)} %all_to_all.40, bf16[384,4096]{1,0:T(8,128)(2,1)S(1)} %copy-done, pred[384]{0:T(512)(128)(4,1)S(1)} %broadcast_compare_fusion), kind=kOutput, calls=%fused_computation.15 | convolution fusion | flops 2013757440 | bytes 9372032 | tf_op jit(solution)/shard_map/dot_general | solution.py:107
  (20 shorter events, 0.2 us)
Async XLA Ops:
  7.2 456.8 %copy-start = (bf16[384,4096]{1,0:T(8,128)(2,1)S(1)}, bf16[384,4096]{1,0:T(8,128)(2,1)}, u32[]{:S(2)}) copy-start(bf16[384,4096]{1,0:T(8,128)(2,1)} %param.23) | copy-start | bytes 9437188
  7.2 127.4 %all-gather.2.cloned.1.call-start = ((), (), s32[]{:S(2)}) async-start(), calls=%async_computation.7 | async-start | bytes 11206656 | tf_op jit(solution)/shard_map/all_gather | solution.py:71
  80.4 146.6 %reduce-scatter.2.cloned.1.call-start = ((), (), s32[]{:S(2)}) async-start(), calls=%async_computation.8 | async-start | bytes 11206656 | tf_op jit(solution)/shard_map/reduce_scatter | solution.py:89
  134.6 8.6 %copy-start.2 = (bf16[1,1216,192]{1,2,0:T(8,128)(2,1)S(1)}, bf16[1,1216,192]{1,2,0:T(8,128)(2,1)}, u32[]{:S(2)}) copy-start(bf16[1,1216,192]{1,2,0:T(8,128)(2,1)} %param.18) | copy-start | bytes 1400836
  134.6 8.6 %copy-start.3 = (bf16[1,4096,192]{1,2,0:T(8,128)(2,1)S(1)}, bf16[1,4096,192]{1,2,0:T(8,128)(2,1)}, u32[]{:S(2)}) copy-start(bf16[1,4096,192]{1,2,0:T(8,128)(2,1)} %param.20) | copy-start | bytes 4718596
  134.6 8.6 %copy-start.5 = (bf16[1,1216,192]{1,2,0:T(8,128)(2,1)S(1)}, bf16[1,1216,192]{1,2,0:T(8,128)(2,1)}, u32[]{:S(2)}) copy-start(bf16[1,1216,192]{1,2,0:T(8,128)(2,1)} %param.19) | copy-start | bytes 1400836
  142.2 0.9 copy-start.1
  165.7 0.9 copy-start.4
  167.3 62.0 %all-to-all-start = ((f32[8,1,128]{2,1,0:T(1,128)}), f32[8,1,128]{2,1,0:T(1,128)S(1)}, u32[]{:S(2)}, u32[]{:S(2)}) async-start(f32[8,1,128]{2,1,0:T(1,128)} %broadcast_in_dim.16), calls=%async_computation | async-start | bytes 8192 | tf_op jit(solution)/shard_map/all_to_all | solution.py:18
  229.3 44.7 %all-to-all-start.2 = ((bf16[32,38,512]{2,1,0:T(8,128)(2,1)}), bf16[32,38,512]{2,1,0:T(8,128)(2,1)}, u32[]{:S(2)}, u32[]{:S(2)}) async-start(bf16[32,38,512]{2,1,0:T(8,128)(2,1)} %all_to_all.35), calls=%async_computation.3 | async-start | bytes 2621440 | tf_op jit(solution)/shard_map/all_to_all | solution.py:92
  283.6 2.1 copy-start.7
  286.5 8.9 %all-to-all-start.3 = ((f32[8,1,128]{2,1,0:T(1,128)}), f32[8,1,128]{2,1,0:T(1,128)S(1)}, u32[]{:S(2)}, u32[]{:S(2)}) async-start(f32[8,1,128]{2,1,0:T(1,128)} %broadcast_in_dim.18), calls=%async_computation.4 | async-start | bytes 8192 | tf_op jit(solution)/shard_map/all_to_all | solution.py:18
  296.5 9.4 %copy-start.6 = (bf16[128,512]{1,0:T(8,128)(2,1)}, bf16[128,512]{1,0:T(8,128)(2,1)S(1)}, u32[]{:S(2)}) copy-start(bf16[128,512]{1,0:T(8,128)(2,1)S(1)} %fusion.34) | copy-start | bytes 393220
  309.4 6.1 %copy-start.8 = (s32[384]{0:T(512)S(1)}, s32[384]{0:T(512)}, u32[]{:S(2)}) copy-start(s32[384]{0:T(512)} %param.24) | copy-start | bytes 4612
  309.4 146.7 %all-to-all-start.5 = ((bf16[32,20,4096]{2,1,0:T(8,128)(2,1)}), bf16[32,20,4096]{2,1,0:T(8,128)(2,1)}, u32[]{:S(2)}, u32[]{:S(2)}) async-start(bf16[32,20,4096]{2,1,0:T(8,128)(2,1)} %tile.9), calls=%async_computation.6 | async-start | bytes 12582912 | tf_op jit(solution)/shard_map/all_to_all | solution.py:13
Sparse Core Ops, SparseCore 0:
  80.5 54.0 all-gather.1
  165.9 61.0 reduce-scatter.1
